TPU v7x, 32 devices: a whole 2x2x4 slice. The times are simulated.
32 devices in a mesh: rows: 16 (over z, y, x), trees: 2 (over core).
Axes of the slice: x: 2, y: 2, z: 4, core: 2. Of those that a mesh axis runs over, the one named last changes fastest.
Arguments:
- tiles: bfloat16 [2, 16, 4, 256, 256], P('trees', 'rows'), may hold values from -0.0625 to 0.0625
- tile_src: int32 [2, 16, 4], P('trees', 'rows'), may hold values from 0 to 3, as said below
- tile_dst: int32 [2, 16, 4], P('trees', 'rows'), may hold values from 0 to 1
- leaf_rhs: bfloat16 [2, 16, 256, 128], P('trees', 'rows'), may hold values from -6 to 6
- leaf_inv: bfloat16 [2, 16, 256, 256], P('trees', 'rows'), may hold values from -0.375 to 0.375
- leaf_owner: int32 [2, 2], P('trees'), may hold values from 0 to 15, as said below
- anc_rhs: bfloat16 [2, 16, 256, 128], P('trees', 'rows'), may hold values from -5 to 5
- anc_inv: bfloat16 [16, 256, 256], P('rows'), may hold values from -0.25 to 0.25
- anc_owner: int32 [4], replicated, may hold values from 0 to 15, as said below
Outputs:
- solved: bfloat16 [4, 256, 128], P(None, None, 'rows')
Inputs may be any that keep to these rules, and one draw needn't show every extreme that they name: `leaf_owner`: the 2 owners of one subtree differ. `anc_owner`: all owners differ. `tile_src`: a tile of wave w names a block below 2 * w.
All inputs are finite; a program needn't handle non-finite values.
Results may differ from a plain program's by a relative error of at most 0.011.
Values may be sent and summed in bfloat16 or wider, within the bound.
A program may use at most 64 MiB of HBM per device.

v0:
```python
import functools

import jax
import jax.numpy as jnp
from jax import lax
from jax.experimental import pallas as pl
from jax.experimental.pallas import tpu as pltpu
from jax.sharding import PartitionSpec as P

WAVES = 3
WB = 2
TW = 2
MESH = pl.DeviceIdType.MESH
F32 = jnp.float32
BF16 = jnp.bfloat16


def broadcast(block, axis, source):
    block = jnp.where(lax.axis_index(axis) == source, block, jnp.zeros_like(block))
    return lax.psum(block, axis)


def general_body(tiles, tile_src, tile_dst, leaf_rhs, leaf_inv, leaf_owner, anc_rhs, anc_inv, anc_owner):
    row_count = lax.axis_size("rows")
    here = lax.axis_index("rows")
    share = leaf_rhs.shape[-1] // row_count
    own_leaf = jnp.dot(leaf_inv[0, 0], leaf_rhs[0, 0], preferred_element_type=F32).astype(BF16)
    known = []
    for block in range(WB):
        known.append(broadcast(own_leaf, "rows", leaf_owner[0, block]))
    outputs = []
    for wave in range(1, WAVES):
        start = (wave - 1) * TW
        sources = jnp.stack(known)
        block_tiles = tiles[0, 0, start : start + TW]
        picked = jnp.take(sources, tile_src[0, 0, start : start + TW], axis=0)
        product = jnp.einsum("kij,kjr->kir", block_tiles, picked, preferred_element_type=F32)
        onehot = (
            tile_dst[0, 0, start : start + TW][:, None] == jnp.arange(WB, dtype=jnp.int32)[None, :]
        ).astype(F32)
        owners = anc_owner[(wave - 1) * WB : wave * WB]
        mine = (owners == here).astype(F32)
        partial_value = mine[:, None, None] * anc_rhs[0, 0].astype(F32)[None] - jnp.einsum(
            "kb,kir->bir", onehot, product
        )
        summed = lax.psum(partial_value, ("rows", "trees"))
        chosen = jnp.einsum("b,bir->ir", mine, summed).astype(BF16)
        local_x = jnp.dot(anc_inv[0], chosen, preferred_element_type=F32).astype(BF16)
        for block in range(WB):
            result = broadcast(local_x, "rows", owners[block])
            known.append(result)
            outputs.append(lax.dynamic_slice_in_dim(result, here * share, share, 1))
    return jnp.stack(outputs)


NT = (((1,), (1,)), ((), ()))


def kernel(
    n, nt, tiles_h, src, dst, rhs_h, linv_h, lown, arhs_h, ainv_h, aown, out,
    tiles, rhs, linv, arhs, ainv, own, leaf_rs, leaf_ag, inv_rs, inv_half, inv_ag, known, u_send, u_recv, xs,
    lsem, ssem, rsem,
):
    r = lax.axis_index("rows")
    t = lax.axis_index("trees")
    depth = rhs.shape[0]
    count = rhs.shape[1]
    ch = depth // n
    share = count // n
    every = n * nt

    def partner(m):
        if n & (n - 1):
            return lax.rem(r + m, n)
        j = r
        bit = 1
        while bit < n:
            if m & bit:
                j = j + bit * (1 - 2 * lax.rem(r // bit, 2))
            bit *= 2
        return j

    inner = 1
    while inner * inner * 4 <= n and n % (inner * 2) == 0:
        inner *= 2
    masks = sorted(range(1, n), key=lambda m: (-(m // inner + m % inner), m // inner))
    others = [partner(m) for m in masks]
    everyone = [(j, q) for j in others for q in (t, 1 - t)] + [(r, 1 - t)]

    barrier = pltpu.get_barrier_semaphore()
    for where in everyone:
        pl.semaphore_signal(barrier, inc=1, device_id=where, device_id_type=MESH)

    loads = []
    for i, (a, b) in enumerate(
        ((linv_h.at[0, 0], linv), (rhs_h.at[0, 0], rhs), (ainv_h.at[0], ainv), (arhs_h.at[0, 0], arhs), (tiles_h.at[0, 0], tiles))
    ):
        c = pltpu.make_async_copy(a, b, lsem.at[i])
        c.start()
        loads.append(c)
    loads[0].wait()
    loads[1].wait()
    own_leaf = jnp.dot(linv[...], rhs[...], preferred_element_type=F32)
    own[...] = own_leaf.T.astype(BF16).reshape(n, share, depth)
    loads[2].wait()
    pl.semaphore_wait(barrier, every - 1)

    def rows_send(phase, make):
        for j in others:
            a, b = make(j)
            pltpu.make_async_remote_copy(
                src_ref=a, dst_ref=b, send_sem=ssem.at[phase], recv_sem=rsem.at[phase],
                device_id=(j, t), device_id_type=MESH,
            ).start()

    def all_send(phase, make):
        for pr, pt in everyone:
            a, b = make(pr, pt)
            pltpu.make_async_remote_copy(
                src_ref=a, dst_ref=b, send_sem=ssem.at[phase], recv_sem=rsem.at[phase],
                device_id=(pr, pt), device_id_type=MESH,
            ).start()

    def landed(phase, view):
        pltpu.make_async_copy(view, view, rsem.at[phase]).wait()

    def sent(phase, view):
        pltpu.make_async_copy(view, view, ssem.at[phase]).wait()

    most = pl.ds(0, n - 1)
    outer = n // inner
    ro, ri = r // inner, lax.rem(r, inner)
    chunk = ri * outer + ro
    lanes_each = depth // nt
    lanes = pl.ds(pl.multiple_of(t * lanes_each, lanes_each), lanes_each)

    def inv_part(j):
        at = (lax.rem(j, inner) * outer + j // inner) * ch
        return pl.ds(pl.multiple_of(at, ch), ch)

    def push(phase, a, b, where):
        pltpu.make_async_remote_copy(
            src_ref=a, dst_ref=b, send_sem=ssem.at[phase], recv_sem=rsem.at[phase],
            device_id=where, device_id_type=MESH,
        ).start()

    def inner_send(w, phase):
        held = pl.ds(ri * outer, outer)
        for k in range(1, inner):
            to = ro * inner + lax.rem(ri + k, inner)
            push(phase, inv_ag.at[w, held], inv_ag.at[w, held], (to, t))

    inner_view = inv_ag.at[0, pl.ds(0, (inner - 1) * outer)]
    outer_view = inv_ag.at[0, pl.ds(0, (outer - 1) * (WAVES - 1))]
    last = 4 + 3 * (WAVES - 1)
    swap = last + 1
    rows_send(0, lambda j: (own.at[j], leaf_rs.at[r]))
    leaf_rs[r] = own[r]
    rows_send(1, lambda j: (ainv.at[inv_part(j), lanes], inv_rs.at[r]))
    inv_rs[r] = ainv[inv_part(r), lanes]

    landed(0, leaf_rs.at[most])
    for b in range(WB):
        leaf_ag[r, b] = leaf_rs[lown[0, b]]
    rows_send(2, lambda j: (leaf_ag.at[r], leaf_ag.at[r]))
    landed(1, inv_rs.at[most])
    for w in range(WAVES - 1):
        inv_half[w] = inv_rs[aown[w * WB + 1 - t]]
        push(swap, inv_half.at[w], inv_ag.at[w, chunk, :, lanes], (r, 1 - t))
    for w in range(WAVES - 1):
        inv_ag[w, chunk, :, lanes] = inv_rs[aown[w * WB + t]]
    landed(swap, inv_half)
    for k in range(1, outer):
        to = lax.rem(ro + k, outer) * inner + ri
        for w in range(WAVES - 1):
            push(3, inv_ag.at[w, chunk], inv_ag.at[w, chunk], (to, t))

    loads[3].wait()
    loads[4].wait()
    arhs_t = arhs[...].astype(F32).T
    landed(2, leaf_ag.at[most])
    for b in range(WB):
        known[b] = leaf_ag[:, b].reshape(count, depth)

    for w in range(WAVES - 1):
        up = 4 + 3 * w
        products = []
        for k in range(w * TW, (w + 1) * TW):
            products.append(
                lax.dot_general(known[src[0, 0, k]], tiles[k], NT, preferred_element_type=F32)
            )
        for b in range(WB):
            part = jnp.where(aown[w * WB + b] == r, arhs_t, 0.0)
            for k in range(TW):
                part = part - jnp.where(dst[0, 0, w * TW + k] == b, products[k], 0.0)
            u_send[w, b] = part.reshape(n, share, depth).astype(BF16)
        all_send(up, lambda pr, pt: (u_send.at[w, pt, pr], u_recv.at[w, r * nt + t]))
        u_recv[w, r * nt + t] = u_send[w, t, r]
        if w == 0:
            landed(3, outer_view)
            inner_send(0, up + 1)
        landed(up, u_recv.at[w, pl.ds(0, every - 1)])
        y = jnp.sum(u_recv[w].astype(F32), axis=0).astype(BF16)
        landed(up + 1, inner_view)
        inv = inv_ag[w].reshape(depth, depth)
        x = lax.dot_general(y, inv, NT, preferred_element_type=F32).astype(BF16)
        xs[w, t, r] = x
        if w + 1 < WAVES - 1:
            all_send(up + 2, lambda pr, pt: (xs.at[w, t, r], xs.at[w, t, r]))
            inner_send(w + 1, up + 4)
            landed(up + 2, u_recv.at[w, pl.ds(0, every - 1)])
            for b in range(WB):
                known[(w + 1) * WB + b] = xs[w, b].reshape(count, depth)
        else:
            pltpu.make_async_remote_copy(
                src_ref=xs.at[w, t, r], dst_ref=xs.at[w, t, r], send_sem=ssem.at[last],
                recv_sem=rsem.at[last], device_id=(r, 1 - t), device_id_type=MESH,
            ).start()
            landed(last, xs.at[w, 0, 0])
    for w in range(WAVES - 1):
        for b in range(WB):
            out[w * WB + b] = xs[w, b, r]

    sent(0, own.at[most])
    sent(1, inv_rs.at[most])
    sent(2, leaf_ag.at[most])
    sent(3, outer_view)
    sent(swap, inv_half)
    sent(last, xs.at[0, 0, 0])
    for w in range(WAVES - 1):
        up = 4 + 3 * w
        sent(up, u_recv.at[w, pl.ds(0, every - 1)])
        sent(up + 1, inner_view)
        if w + 1 < WAVES - 1:
            sent(up + 2, u_recv.at[w, pl.ds(0, every - 1)])


def fast_body(n, nt, tiles, tile_src, tile_dst, leaf_rhs, leaf_inv, leaf_owner, anc_rhs, anc_inv, anc_owner):
    depth, count = leaf_rhs.shape[-2:]
    kinds = tiles.shape[2]
    ch, share, every = depth // n, count // n, n * nt
    waves = WAVES - 1
    phases = 6 + 3 * waves
    any_spec = pl.BlockSpec(memory_space=pl.ANY)
    smem = pl.BlockSpec(memory_space=pltpu.SMEM)
    found = pl.pallas_call(
        functools.partial(kernel, n, nt),
        out_shape=jax.ShapeDtypeStruct((waves * WB, share, depth), BF16),
        in_specs=[any_spec, smem, smem, any_spec, any_spec, smem, any_spec, any_spec, smem],
        out_specs=pl.BlockSpec(memory_space=pltpu.VMEM),
        scratch_shapes=[
            pltpu.VMEM((kinds, depth, depth), BF16),
            pltpu.VMEM((depth, count), BF16),
            pltpu.VMEM((depth, depth), BF16),
            pltpu.VMEM((depth, count), BF16),
            pltpu.VMEM((depth, depth), BF16),
            pltpu.VMEM((n, share, depth), BF16),
            pltpu.VMEM((n, share, depth), BF16),
            pltpu.VMEM((n, WB, share, depth), BF16),
            pltpu.VMEM((n, ch, depth // nt), BF16),
            pltpu.VMEM((waves, ch, depth // nt), BF16),
            pltpu.VMEM((waves, n, ch, depth), BF16),
            pltpu.VMEM((WB * waves, count, depth), BF16),
            pltpu.VMEM((waves, WB, n, share, depth), BF16),
            pltpu.VMEM((waves, every, share, depth), BF16),
            pltpu.VMEM((waves, WB, n, share, depth), BF16),
            pltpu.SemaphoreType.DMA((5,)),
            pltpu.SemaphoreType.DMA((phases,)),
            pltpu.SemaphoreType.DMA((phases,)),
        ],
        compiler_params=pltpu.CompilerParams(collective_id=0, has_side_effects=True),
    )(tiles, tile_src, tile_dst, leaf_rhs, leaf_inv, leaf_owner, anc_rhs, anc_inv, anc_owner)
    return jnp.swapaxes(found, 1, 2)


def solution(mesh):
    n, nt = mesh.shape["rows"], mesh.shape["trees"]
    placed = (
        P("trees", "rows", None, None, None),
        P("trees", "rows", None),
        P("trees", "rows", None),
        P("trees", "rows", None, None),
        P("trees", "rows", None, None),
        P("trees", None),
        P("trees", "rows", None, None),
        P("rows", None, None),
        P(),
    )

    def body(*args):
        depth, count = args[3].shape[-2:]
        if nt == WB and n > 3 and depth % (16 * n) == 0 and depth % (128 * nt) == 0 and count % (8 * n) == 0:
            return fast_body(n, nt, *args)
        return general_body(*args)

    return jax.shard_map(
        body, mesh=mesh, in_specs=placed, out_specs=P(None, None, "rows"), check_vma=False
    )
```

profile of v0, /device:TPU:0, one launch (start us, length us, event | category | flops | bytes accessed | tf_op | source)
XLA Modules:
  0.0 35.1 jit_solution(16118560547811857037)
XLA Ops:
  0.0 33.8 %shard_map.91 = bf16[4,8,256]{2,1,0:T(8,128)(2,1)} custom-call(bf16[1,1,4,256,256]{4,3,2,1,0:T(8,128)(2,1)} %tiles_h.1, s32[1,1,4]{2,1,0:T(1,128)} %src.1, s32[1,1,4]{2,1,0:T(1,128)} %dst.1, bf16[1,1,256,128]{3,2,1,0:T(8,128)(2,1)} %rhs_h.1, bf16[1,1,256,256]{3,2,1,0:T(8,128)(2,1)} %linv_h.1, s32[1,2]{1,0:T(1,128)} %lown.1, bf16[1,1,256,128]{3,2,1,0:T(8,128)(2,1)} %arhs_h.1, ...), custom_call_target="tpu_custom_call" | custom-call | tf_op jit(solution)/shard_map/pallas_call | solution.py:246
  33.8 1.3 %copy.11 = bf16[4,256,8]{1,2,0:T(8,128)(2,1)} copy(bf16[4,256,8]{1,2,0:T(8,128)(2,1)} %bitcast.1) | data formatting | bytes 32768
where the time goes:
time: 35.4 us; the launch traced here: 35.1 us
  Pallas kernels  33.8 us (95%)
  local copies, waits for them, and re-layouts  1.32 us (4%)
    pallas_call x1, Pallas kernels, fast_body(): pl.pallas_call(functools.partial(kernel, n, nt), out_shape=jax.ShapeDtype...  33.8 us
    unnamed x1, local copies, waits for them, and re-layouts  1.32 us

commit v1 on v0

--- a/solution.py
+++ b/solution.py
@@ -59,7 +59,7 @@
 def kernel(
     n, nt, tiles_h, src, dst, rhs_h, linv_h, lown, arhs_h, ainv_h, aown, out,
     tiles, rhs, linv, arhs, ainv, own, leaf_rs, leaf_ag, inv_rs, inv_half, inv_ag, known, u_send, u_recv, xs,
-    lsem, ssem, rsem,
+    u_mine, u_other, coef, coef_rs, mat_rs, mat_send, mat_recv, mat_sum, mat_ag, lsem, ssem, rsem,
 ):
     r = lax.axis_index("rows")
     t = lax.axis_index("trees")
@@ -98,28 +98,28 @@
         c = pltpu.make_async_copy(a, b, lsem.at[i])
         c.start()
         loads.append(c)
+    for k in range(TW):
+        for b in range(WB):
+            for s in range(WB):
+                hit = (dst[0, 0, TW + k] == b) & (src[0, 0, TW + k] == WB + s)
+                coef[(k * WB + b) * WB + s] = jnp.full((128,), jnp.where(hit, 1.0, 0.0), F32)
     loads[0].wait()
     loads[1].wait()
     own_leaf = jnp.dot(linv[...], rhs[...], preferred_element_type=F32)
     own[...] = own_leaf.T.astype(BF16).reshape(n, share, depth)
     loads[2].wait()
+    loads[4].wait()
     pl.semaphore_wait(barrier, every - 1)
+
+    def push(phase, a, b, where):
+        pltpu.make_async_remote_copy(
+            src_ref=a, dst_ref=b, send_sem=ssem.at[phase], recv_sem=rsem.at[phase],
+            device_id=where, device_id_type=MESH,
+        ).start()
 
     def rows_send(phase, make):
         for j in others:
-            a, b = make(j)
-            pltpu.make_async_remote_copy(
-                src_ref=a, dst_ref=b, send_sem=ssem.at[phase], recv_sem=rsem.at[phase],
-                device_id=(j, t), device_id_type=MESH,
-            ).start()
-
-    def all_send(phase, make):
-        for pr, pt in everyone:
-            a, b = make(pr, pt)
-            pltpu.make_async_remote_copy(
-                src_ref=a, dst_ref=b, send_sem=ssem.at[phase], recv_sem=rsem.at[phase],
-                device_id=(pr, pt), device_id_type=MESH,
-            ).start()
+            push(phase, *make(j), (j, t))
 
     def landed(phase, view):
         pltpu.make_async_copy(view, view, rsem.at[phase]).wait()
@@ -134,105 +134,151 @@
     lanes_each = depth // nt
     lanes = pl.ds(pl.multiple_of(t * lanes_each, lanes_each), lanes_each)
 
+    def rows_of(at):
+        return pl.ds(pl.multiple_of(at * ch, ch), ch)
+
     def inv_part(j):
-        at = (lax.rem(j, inner) * outer + j // inner) * ch
-        return pl.ds(pl.multiple_of(at, ch), ch)
-
-    def push(phase, a, b, where):
-        pltpu.make_async_remote_copy(
-            src_ref=a, dst_ref=b, send_sem=ssem.at[phase], recv_sem=rsem.at[phase],
-            device_id=where, device_id_type=MESH,
-        ).start()
-
-    def inner_send(w, phase):
+        return rows_of(lax.rem(j, inner) * outer + j // inner)
+
+    def inner_send(w):
         held = pl.ds(ri * outer, outer)
         for k in range(1, inner):
             to = ro * inner + lax.rem(ri + k, inner)
-            push(phase, inv_ag.at[w, held], inv_ag.at[w, held], (to, t))
+            push(INV_IN + w, inv_ag.at[w, held], inv_ag.at[w, held], (to, t))
 
     inner_view = inv_ag.at[0, pl.ds(0, (inner - 1) * outer)]
     outer_view = inv_ag.at[0, pl.ds(0, (outer - 1) * (WAVES - 1))]
-    last = 4 + 3 * (WAVES - 1)
-    swap = last + 1
-    rows_send(0, lambda j: (own.at[j], leaf_rs.at[r]))
+    (LEAF_RS, INV_RS, LEAF_AG, INV_OUT, INV_SWAP, COEF, MAT_RS, MAT_ZRS, MAT_ZAG, MAT_AG, X1, X2, INV_IN, _,
+     UP, _, US, _) = range(18)
+    zs = [lax.rem(ro + k, outer) for k in range(1, outer)]
+    near = [(lax.rem(ri + k, inner), q) for k in range(1, inner) for q in (t, 1 - t)] + [(ri, 1 - t)]
+    place = ri * nt + t
+    part = depth // (inner * nt)
+    piece = part // outer
+    rows_send(LEAF_RS, lambda j: (own.at[j], leaf_rs.at[r]))
     leaf_rs[r] = own[r]
-    rows_send(1, lambda j: (ainv.at[inv_part(j), lanes], inv_rs.at[r]))
+    second = pl.ds(TW, TW)
+
+    def mat_rows(i, q):
+        return pl.ds(pl.multiple_of((i * nt + q) * part, part), part)
+
+    for i, q in near:
+        push(COEF, coef, coef_rs.at[place], (ro * inner + i, q))
+        push(MAT_RS, tiles.at[second, mat_rows(i, q)], mat_rs.at[place], (ro * inner + i, q))
+    coef_rs[place] = coef[...]
+    mat_rs[place] = tiles[second, mat_rows(ri, t)]
+    rows_send(INV_RS, lambda j: (ainv.at[inv_part(j), lanes], inv_rs.at[r]))
     inv_rs[r] = ainv[inv_part(r), lanes]
 
-    landed(0, leaf_rs.at[most])
+    landed(LEAF_RS, leaf_rs.at[most])
     for b in range(WB):
         leaf_ag[r, b] = leaf_rs[lown[0, b]]
-    rows_send(2, lambda j: (leaf_ag.at[r], leaf_ag.at[r]))
-    landed(1, inv_rs.at[most])
+    rows_send(LEAF_AG, lambda j: (leaf_ag.at[r], leaf_ag.at[r]))
+
+    landed(COEF, coef_rs.at[pl.ds(0, inner * nt - 1)])
+    landed(MAT_RS, mat_rs.at[pl.ds(0, inner * nt - 1)])
+    slots = [[jnp.zeros((part, depth), F32) for s in range(WB)] for b in range(WB)]
+    for j in range(inner * nt):
+        for k in range(TW):
+            value = mat_rs[j, k].astype(F32)
+            for b in range(WB):
+                for s in range(WB):
+                    at = (k * WB + b) * WB + s
+                    scale = coef_rs[j, at : at + 1]
+                    scale = jnp.concatenate([scale] * (depth // 128), axis=1)
+                    slots[b][s] = slots[b][s] + scale * value
+    for b in range(WB):
+        for s in range(WB):
+            mat_send[:, b, s] = slots[b][s].reshape(outer, piece, depth).astype(BF16)
+    for z in zs:
+        push(MAT_ZRS, mat_send.at[z], mat_recv.at[ro], (z * inner + ri, t))
+    mat_recv[ro] = mat_send[ro]
+
+    landed(INV_RS, inv_rs.at[most])
     for w in range(WAVES - 1):
         inv_half[w] = inv_rs[aown[w * WB + 1 - t]]
-        push(swap, inv_half.at[w], inv_ag.at[w, chunk, :, lanes], (r, 1 - t))
+        push(INV_SWAP, inv_half.at[w], inv_ag.at[w, chunk, :, lanes], (r, 1 - t))
     for w in range(WAVES - 1):
         inv_ag[w, chunk, :, lanes] = inv_rs[aown[w * WB + t]]
-    landed(swap, inv_half)
-    for k in range(1, outer):
-        to = lax.rem(ro + k, outer) * inner + ri
+    loads[3].wait()
+    arhs_t = arhs[...].astype(F32).T
+    landed(INV_SWAP, inv_half)
+    for z in zs:
         for w in range(WAVES - 1):
-            push(3, inv_ag.at[w, chunk], inv_ag.at[w, chunk], (to, t))
-
-    loads[3].wait()
-    loads[4].wait()
-    arhs_t = arhs[...].astype(F32).T
-    landed(2, leaf_ag.at[most])
+            push(INV_OUT, inv_ag.at[w, chunk], inv_ag.at[w, chunk], (z * inner + ri, t))
+
+    landed(MAT_ZRS, mat_recv.at[pl.ds(0, outer - 1)])
+    mat_sum[:, ro] = jnp.sum(mat_recv[...].astype(F32), axis=0).astype(BF16)
+    for z in zs:
+        push(MAT_ZAG, mat_sum.at[:, ro], mat_sum.at[:, ro], (z * inner + ri, t))
+
+    landed(LEAF_AG, leaf_ag.at[most])
     for b in range(WB):
         known[b] = leaf_ag[:, b].reshape(count, depth)
-
-    for w in range(WAVES - 1):
-        up = 4 + 3 * w
+    for w in range(WAVES - 1):
         products = []
         for k in range(w * TW, (w + 1) * TW):
-            products.append(
-                lax.dot_general(known[src[0, 0, k]], tiles[k], NT, preferred_element_type=F32)
-            )
+            from_leaf = known[jnp.minimum(src[0, 0, k], WB - 1)]
+            products.append(lax.dot_general(from_leaf, tiles[k], NT, preferred_element_type=F32))
         for b in range(WB):
-            part = jnp.where(aown[w * WB + b] == r, arhs_t, 0.0)
+            u = jnp.where(aown[w * WB + b] == r, arhs_t, 0.0)
             for k in range(TW):
-                part = part - jnp.where(dst[0, 0, w * TW + k] == b, products[k], 0.0)
-            u_send[w, b] = part.reshape(n, share, depth).astype(BF16)
-        all_send(up, lambda pr, pt: (u_send.at[w, pt, pr], u_recv.at[w, r * nt + t]))
-        u_recv[w, r * nt + t] = u_send[w, t, r]
-        if w == 0:
-            landed(3, outer_view)
-            inner_send(0, up + 1)
-        landed(up, u_recv.at[w, pl.ds(0, every - 1)])
-        y = jnp.sum(u_recv[w].astype(F32), axis=0).astype(BF16)
-        landed(up + 1, inner_view)
+                hit = (dst[0, 0, w * TW + k] == b) & (src[0, 0, w * TW + k] < WB)
+                u = u - jnp.where(hit, products[k], 0.0)
+            u_mine[w, b] = u.astype(BF16)
+        push(US + w, u_mine.at[w, 1 - t], u_other.at[w], (r, 1 - t))
+    landed(INV_OUT, outer_view)
+    inner_send(0)
+    for w in range(WAVES - 1):
+        landed(US + w, u_other.at[w])
+        u = u_mine[w, t].astype(F32) + u_other[w].astype(F32)
+        u_send[w] = u.reshape(n, share, depth).astype(BF16)
+        rows_send(UP + w, lambda j: (u_send.at[w, j], u_recv.at[w, r]))
+        u_recv[w, r] = u_send[w, r]
+    landed(MAT_ZAG, mat_sum.at[:, pl.ds(0, outer - 1)])
+    for i, q in near:
+        push(MAT_AG, mat_sum.at[q], mat_ag.at[place], (ro * inner + i, q))
+    mat_ag[place] = mat_sum[t]
+    inner_send(1)
+
+    def solve(w, y):
         inv = inv_ag[w].reshape(depth, depth)
-        x = lax.dot_general(y, inv, NT, preferred_element_type=F32).astype(BF16)
-        xs[w, t, r] = x
-        if w + 1 < WAVES - 1:
-            all_send(up + 2, lambda pr, pt: (xs.at[w, t, r], xs.at[w, t, r]))
-            inner_send(w + 1, up + 4)
-            landed(up + 2, u_recv.at[w, pl.ds(0, every - 1)])
-            for b in range(WB):
-                known[(w + 1) * WB + b] = xs[w, b].reshape(count, depth)
-        else:
-            pltpu.make_async_remote_copy(
-                src_ref=xs.at[w, t, r], dst_ref=xs.at[w, t, r], send_sem=ssem.at[last],
-                recv_sem=rsem.at[last], device_id=(r, 1 - t), device_id_type=MESH,
-            ).start()
-            landed(last, xs.at[w, 0, 0])
+        xs[w, t] = lax.dot_general(y.astype(BF16), inv, NT, preferred_element_type=F32).astype(BF16)
+        push(X1 + w, xs.at[w, t], xs.at[w, t], (r, 1 - t))
+
+    landed(UP, u_recv.at[0, most])
+    y = jnp.sum(u_recv[0].astype(F32), axis=0)
+    landed(INV_IN, inner_view)
+    solve(0, y)
+    landed(UP + 1, u_recv.at[1, most])
+    y = jnp.sum(u_recv[1].astype(F32), axis=0)
+    landed(MAT_AG, mat_ag.at[pl.ds(0, inner * nt - 1)])
+    landed(INV_IN + 1, inner_view)
+    landed(X1, xs.at[0, 0])
+    for s in range(WB):
+        mat = mat_ag[:, :, s].reshape(depth, depth)
+        y = y - lax.dot_general(xs[0, s], mat, NT, preferred_element_type=F32)
+    solve(1, y)
+    landed(X2, xs.at[0, 0])
     for w in range(WAVES - 1):
         for b in range(WB):
-            out[w * WB + b] = xs[w, b, r]
-
-    sent(0, own.at[most])
-    sent(1, inv_rs.at[most])
-    sent(2, leaf_ag.at[most])
-    sent(3, outer_view)
-    sent(swap, inv_half)
-    sent(last, xs.at[0, 0, 0])
-    for w in range(WAVES - 1):
-        up = 4 + 3 * w
-        sent(up, u_recv.at[w, pl.ds(0, every - 1)])
-        sent(up + 1, inner_view)
-        if w + 1 < WAVES - 1:
-            sent(up + 2, u_recv.at[w, pl.ds(0, every - 1)])
+            out[w * WB + b] = xs[w, b]
+
+    sent(LEAF_RS, own.at[most])
+    sent(INV_RS, inv_rs.at[most])
+    sent(COEF, coef_rs.at[pl.ds(0, inner * nt - 1)])
+    sent(MAT_RS, mat_rs.at[pl.ds(0, inner * nt - 1)])
+    sent(LEAF_AG, leaf_ag.at[most])
+    sent(INV_OUT, outer_view)
+    sent(INV_SWAP, inv_half)
+    sent(MAT_ZRS, mat_recv.at[pl.ds(0, outer - 1)])
+    sent(MAT_ZAG, mat_sum.at[:, pl.ds(0, outer - 1)])
+    sent(MAT_AG, mat_ag.at[pl.ds(0, inner * nt - 1)])
+    for w in range(WAVES - 1):
+        sent(US + w, u_other.at[w])
+        sent(UP + w, u_recv.at[w, most])
+        sent(INV_IN + w, inner_view)
+        sent(X1 + w, xs.at[0, 0])
 
 
 def fast_body(n, nt, tiles, tile_src, tile_dst, leaf_rhs, leaf_inv, leaf_owner, anc_rhs, anc_inv, anc_owner):
@@ -240,7 +286,11 @@
     kinds = tiles.shape[2]
     ch, share, every = depth // n, count // n, n * nt
     waves = WAVES - 1
-    phases = 6 + 3 * waves
+    inner = 1
+    while inner * inner * 4 <= n and n % (inner * 2) == 0:
+        inner *= 2
+    outer, part = n // inner, depth // (inner * nt)
+    phases = 18
     any_spec = pl.BlockSpec(memory_space=pl.ANY)
     smem = pl.BlockSpec(memory_space=pltpu.SMEM)
     found = pl.pallas_call(
@@ -261,9 +311,18 @@
             pltpu.VMEM((waves, ch, depth // nt), BF16),
             pltpu.VMEM((waves, n, ch, depth), BF16),
             pltpu.VMEM((WB * waves, count, depth), BF16),
-            pltpu.VMEM((waves, WB, n, share, depth), BF16),
-            pltpu.VMEM((waves, every, share, depth), BF16),
-            pltpu.VMEM((waves, WB, n, share, depth), BF16),
+            pltpu.VMEM((waves, n, share, depth), BF16),
+            pltpu.VMEM((waves, n, share, depth), BF16),
+            pltpu.VMEM((waves, WB, share, depth), BF16),
+            pltpu.VMEM((waves, WB, count, depth), BF16),
+            pltpu.VMEM((waves, count, depth), BF16),
+            pltpu.VMEM((TW * WB * WB, 128), F32),
+            pltpu.VMEM((inner * nt, TW * WB * WB, 128), F32),
+            pltpu.VMEM((inner * nt, TW, part, depth), BF16),
+            pltpu.VMEM((outer, WB, WB, part // outer, depth), BF16),
+            pltpu.VMEM((outer, WB, WB, part // outer, depth), BF16),
+            pltpu.VMEM((WB, outer, WB, part // outer, depth), BF16),
+            pltpu.VMEM((inner * nt, outer, WB, part // outer, depth), BF16),
             pltpu.SemaphoreType.DMA((5,)),
             pltpu.SemaphoreType.DMA((phases,)),
             pltpu.SemaphoreType.DMA((phases,)),
@@ -289,7 +348,7 @@
 
     def body(*args):
         depth, count = args[3].shape[-2:]
-        if nt == WB and n > 3 and depth % (16 * n) == 0 and depth % (128 * nt) == 0 and count % (8 * n) == 0:
+        if WAVES == 3 and nt == WB and n > 3 and depth % (16 * n) == 0 and depth % (128 * nt) == 0 and count % (8 * n) == 0:
             return fast_body(n, nt, *args)
         return general_body(*args)
 

time: 35.4 us -> 32.3 us (0.912)
  Pallas kernels: 33.8 us -> 30.7 us
    pallas_call x1, Pallas kernels: 33.8 us -> 30.7 us  [fast_body(): pl.pallas_call(functools.partial(kernel, n, nt), out_shape=jax.ShapeDtype...]
where the time goes in v1:
time: 32.3 us; the launch traced here: 32.1 us
  Pallas kernels  30.7 us (95%)
  local copies, waits for them, and re-layouts  1.32 us (4%)
    pallas_call x1, Pallas kernels, fast_body(): pl.pallas_call(functools.partial(kernel, n, nt), out_shape=jax.ShapeDtype...  30.7 us
    unnamed x1, local copies, waits for them, and re-layouts  1.32 us

profile of v1, /device:TPU:0, one launch (start us, length us, event | category | flops | bytes accessed | tf_op | source)
XLA Modules:
  0.0 32.1 jit_solution(11186826981711173343)
XLA Ops:
  0.0 30.7 %shard_map.91 = bf16[4,8,256]{2,1,0:T(8,128)(2,1)} custom-call(bf16[1,1,4,256,256]{4,3,2,1,0:T(8,128)(2,1)} %tiles_h.1, s32[1,1,4]{2,1,0:T(1,128)} %src.1, s32[1,1,4]{2,1,0:T(1,128)} %dst.1, bf16[1,1,256,128]{3,2,1,0:T(8,128)(2,1)} %rhs_h.1, bf16[1,1,256,256]{3,2,1,0:T(8,128)(2,1)} %linv_h.1, s32[1,2]{1,0:T(1,128)} %lown.1, bf16[1,1,256,128]{3,2,1,0:T(8,128)(2,1)} %arhs_h.1, ...), custom_call_target="tpu_custom_call" | custom-call | tf_op jit(solution)/shard_map/pallas_call | solution.py:296
  30.7 1.3 %copy.11 = bf16[4,256,8]{1,2,0:T(8,128)(2,1)} copy(bf16[4,256,8]{1,2,0:T(8,128)(2,1)} %bitcast.1) | data formatting | bytes 32768

commit v2 on v1

--- a/solution.py
+++ b/solution.py
@@ -58,8 +58,8 @@
 
 def kernel(
     n, nt, tiles_h, src, dst, rhs_h, linv_h, lown, arhs_h, ainv_h, aown, out,
-    tiles, rhs, linv, arhs, ainv, own, leaf_rs, leaf_ag, inv_rs, inv_half, inv_ag, known, u_send, u_recv, xs,
-    u_mine, u_other, coef, coef_rs, mat_rs, mat_send, mat_recv, mat_sum, mat_ag, lsem, ssem, rsem,
+    tiles, rhs, linv, arhs, ainv, own, leaf_rs, leaf_ag, inv_half, inv_ag, known, u_send, u_recv, xs,
+    u_mine, u_other, mat_src, mat_rs, mat_send, mat_recv, mat_sum, mat_ag, lsem, ssem, rsem,
 ):
     r = lax.axis_index("rows")
     t = lax.axis_index("trees")
@@ -98,17 +98,32 @@
         c = pltpu.make_async_copy(a, b, lsem.at[i])
         c.start()
         loads.append(c)
+    coef = []
     for k in range(TW):
         for b in range(WB):
             for s in range(WB):
                 hit = (dst[0, 0, TW + k] == b) & (src[0, 0, TW + k] == WB + s)
-                coef[(k * WB + b) * WB + s] = jnp.full((128,), jnp.where(hit, 1.0, 0.0), F32)
+                coef.append(jnp.full((1, depth), jnp.where(hit, 1.0, 0.0), F32))
+    coef = jnp.concatenate(coef, axis=0).astype(BF16)
     loads[0].wait()
     loads[1].wait()
     own_leaf = jnp.dot(linv[...], rhs[...], preferred_element_type=F32)
-    own[...] = own_leaf.T.astype(BF16).reshape(n, share, depth)
+    own[:, :share] = own_leaf.T.astype(BF16).reshape(n, share, depth)
     loads[2].wait()
+    half, width = ch // nt, depth // nt
+    lanes0 = pl.ds(pl.multiple_of(t * width, width), width)
+    mine = ainv[:, lanes0]
+    for j in range(n):
+        at = (j % inner) * (n // inner) + j // inner
+        for q in range(nt):
+            own[j, share:, q * width : (q + 1) * width] = mine[at * ch + q * half : at * ch + (q + 1) * half]
     loads[4].wait()
+    pieces = inner * nt
+    part = depth // pieces
+    for j in range(pieces):
+        for k in range(TW):
+            mat_src[j, k * part : (k + 1) * part] = tiles[TW + k, j * part : (j + 1) * part]
+        mat_src[j, TW * part :] = coef
     pl.semaphore_wait(barrier, every - 1)
 
     def push(phase, a, b, where):
@@ -140,16 +155,10 @@
     def inv_part(j):
         return rows_of(lax.rem(j, inner) * outer + j // inner)
 
-    def inner_send(w):
-        held = pl.ds(ri * outer, outer)
-        for k in range(1, inner):
-            to = ro * inner + lax.rem(ri + k, inner)
-            push(INV_IN + w, inv_ag.at[w, held], inv_ag.at[w, held], (to, t))
-
-    inner_view = inv_ag.at[0, pl.ds(0, (inner - 1) * outer)]
-    outer_view = inv_ag.at[0, pl.ds(0, (outer - 1) * (WAVES - 1))]
-    (LEAF_RS, INV_RS, LEAF_AG, INV_OUT, INV_SWAP, COEF, MAT_RS, MAT_ZRS, MAT_ZAG, MAT_AG, X1, X2, INV_IN, _,
-     UP, _, US, _) = range(18)
+    inner_view = inv_ag.at[:, pl.ds(0, (inner - 1) * outer)]
+    outer_view = inv_ag.at[0, pl.ds(0, outer * nt - 1)]
+    (LEAF_RS, INV_RS, LEAF_AG, INV_OUT, _, INV_SWAP, COEF, MAT_RS, MAT_ZRS, MAT_ZAG, MAT_AG, X1, X2, INV_IN, _,
+     UP, _, US, _) = range(19)
     zs = [lax.rem(ro + k, outer) for k in range(1, outer)]
     near = [(lax.rem(ri + k, inner), q) for k in range(1, inner) for q in (t, 1 - t)] + [(ri, 1 - t)]
     place = ri * nt + t
@@ -157,36 +166,36 @@
     piece = part // outer
     rows_send(LEAF_RS, lambda j: (own.at[j], leaf_rs.at[r]))
     leaf_rs[r] = own[r]
-    second = pl.ds(TW, TW)
-
-    def mat_rows(i, q):
-        return pl.ds(pl.multiple_of((i * nt + q) * part, part), part)
-
     for i, q in near:
-        push(COEF, coef, coef_rs.at[place], (ro * inner + i, q))
-        push(MAT_RS, tiles.at[second, mat_rows(i, q)], mat_rs.at[place], (ro * inner + i, q))
-    coef_rs[place] = coef[...]
-    mat_rs[place] = tiles[second, mat_rows(ri, t)]
-    rows_send(INV_RS, lambda j: (ainv.at[inv_part(j), lanes], inv_rs.at[r]))
-    inv_rs[r] = ainv[inv_part(r), lanes]
-
+        push(MAT_RS, mat_src.at[i * nt + q], mat_rs.at[place], (ro * inner + i, q))
+    mat_rs[place] = mat_src[place]
     landed(LEAF_RS, leaf_rs.at[most])
     for b in range(WB):
-        leaf_ag[r, b] = leaf_rs[lown[0, b]]
+        leaf_ag[r, b] = leaf_rs[lown[0, b], :share]
     rows_send(LEAF_AG, lambda j: (leaf_ag.at[r], leaf_ag.at[r]))
 
-    landed(COEF, coef_rs.at[pl.ds(0, inner * nt - 1)])
+    def picked(owner):
+        rows = leaf_rs[owner, share:]
+        return jnp.concatenate([rows[:, q * lanes_each : (q + 1) * lanes_each] for q in range(nt)], axis=0)
+
+    for b in range(WB):
+        for w in range(WAVES - 1):
+            inv_half[b, w] = picked(aown[w * WB + b])
+    for z in zs:
+        for q in (t, 1 - t):
+            push(INV_OUT, inv_half.at[q], inv_ag.at[:, chunk, :, lanes], (z * inner + ri, q))
+    push(INV_OUT, inv_half.at[1 - t], inv_ag.at[:, chunk, :, lanes], (r, 1 - t))
+    inv_ag[:, chunk, :, lanes] = inv_half[t]
     landed(MAT_RS, mat_rs.at[pl.ds(0, inner * nt - 1)])
     slots = [[jnp.zeros((part, depth), F32) for s in range(WB)] for b in range(WB)]
     for j in range(inner * nt):
+        scales = mat_rs[j, TW * part :].astype(F32)
         for k in range(TW):
-            value = mat_rs[j, k].astype(F32)
+            value = mat_rs[j, k * part : (k + 1) * part].astype(F32)
             for b in range(WB):
                 for s in range(WB):
                     at = (k * WB + b) * WB + s
-                    scale = coef_rs[j, at : at + 1]
-                    scale = jnp.concatenate([scale] * (depth // 128), axis=1)
-                    slots[b][s] = slots[b][s] + scale * value
+                    slots[b][s] = slots[b][s] + scales[at : at + 1] * value
     for b in range(WB):
         for s in range(WB):
             mat_send[:, b, s] = slots[b][s].reshape(outer, piece, depth).astype(BF16)
@@ -194,28 +203,22 @@
         push(MAT_ZRS, mat_send.at[z], mat_recv.at[ro], (z * inner + ri, t))
     mat_recv[ro] = mat_send[ro]
 
-    landed(INV_RS, inv_rs.at[most])
-    for w in range(WAVES - 1):
-        inv_half[w] = inv_rs[aown[w * WB + 1 - t]]
-        push(INV_SWAP, inv_half.at[w], inv_ag.at[w, chunk, :, lanes], (r, 1 - t))
-    for w in range(WAVES - 1):
-        inv_ag[w, chunk, :, lanes] = inv_rs[aown[w * WB + t]]
     loads[3].wait()
     arhs_t = arhs[...].astype(F32).T
-    landed(INV_SWAP, inv_half)
-    for z in zs:
-        for w in range(WAVES - 1):
-            push(INV_OUT, inv_ag.at[w, chunk], inv_ag.at[w, chunk], (z * inner + ri, t))
-
     landed(MAT_ZRS, mat_recv.at[pl.ds(0, outer - 1)])
     mat_sum[:, ro] = jnp.sum(mat_recv[...].astype(F32), axis=0).astype(BF16)
     for z in zs:
         push(MAT_ZAG, mat_sum.at[:, ro], mat_sum.at[:, ro], (z * inner + ri, t))
 
+    landed(INV_OUT, outer_view)
+    held = pl.ds(ri * outer, outer)
+    for k in range(1, inner):
+        to = ro * inner + lax.rem(ri + k, inner)
+        push(INV_IN, inv_ag.at[:, held], inv_ag.at[:, held], (to, t))
     landed(LEAF_AG, leaf_ag.at[most])
     for b in range(WB):
         known[b] = leaf_ag[:, b].reshape(count, depth)
-    for w in range(WAVES - 1):
+    for w in (0,):
         products = []
         for k in range(w * TW, (w + 1) * TW):
             from_leaf = known[jnp.minimum(src[0, 0, k], WB - 1)]
@@ -227,9 +230,25 @@
                 u = u - jnp.where(hit, products[k], 0.0)
             u_mine[w, b] = u.astype(BF16)
         push(US + w, u_mine.at[w, 1 - t], u_other.at[w], (r, 1 - t))
-    landed(INV_OUT, outer_view)
-    inner_send(0)
-    for w in range(WAVES - 1):
+    for w in (1,):
+        products = []
+        for k in range(w * TW, (w + 1) * TW):
+            from_leaf = known[jnp.minimum(src[0, 0, k], WB - 1)]
+            products.append(lax.dot_general(from_leaf, tiles[k], NT, preferred_element_type=F32))
+        for b in range(WB):
+            u = jnp.where(aown[w * WB + b] == r, arhs_t, 0.0)
+            for k in range(TW):
+                hit = (dst[0, 0, w * TW + k] == b) & (src[0, 0, w * TW + k] < WB)
+                u = u - jnp.where(hit, products[k], 0.0)
+            u_mine[w, b] = u.astype(BF16)
+        push(US + w, u_mine.at[w, 1 - t], u_other.at[w], (r, 1 - t))
+    for w in (0,):
+        landed(US + w, u_other.at[w])
+        u = u_mine[w, t].astype(F32) + u_other[w].astype(F32)
+        u_send[w] = u.reshape(n, share, depth).astype(BF16)
+        rows_send(UP + w, lambda j: (u_send.at[w, j], u_recv.at[w, r]))
+        u_recv[w, r] = u_send[w, r]
+    for w in (1,):
         landed(US + w, u_other.at[w])
         u = u_mine[w, t].astype(F32) + u_other[w].astype(F32)
         u_send[w] = u.reshape(n, share, depth).astype(BF16)
@@ -239,8 +258,6 @@
     for i, q in near:
         push(MAT_AG, mat_sum.at[q], mat_ag.at[place], (ro * inner + i, q))
     mat_ag[place] = mat_sum[t]
-    inner_send(1)
-
     def solve(w, y):
         inv = inv_ag[w].reshape(depth, depth)
         xs[w, t] = lax.dot_general(y.astype(BF16), inv, NT, preferred_element_type=F32).astype(BF16)
@@ -253,7 +270,6 @@
     landed(UP + 1, u_recv.at[1, most])
     y = jnp.sum(u_recv[1].astype(F32), axis=0)
     landed(MAT_AG, mat_ag.at[pl.ds(0, inner * nt - 1)])
-    landed(INV_IN + 1, inner_view)
     landed(X1, xs.at[0, 0])
     for s in range(WB):
         mat = mat_ag[:, :, s].reshape(depth, depth)
@@ -264,20 +280,17 @@
         for b in range(WB):
             out[w * WB + b] = xs[w, b]
 
+    sent(INV_OUT, outer_view)
+    sent(INV_IN, inner_view)
     sent(LEAF_RS, own.at[most])
-    sent(INV_RS, inv_rs.at[most])
-    sent(COEF, coef_rs.at[pl.ds(0, inner * nt - 1)])
     sent(MAT_RS, mat_rs.at[pl.ds(0, inner * nt - 1)])
     sent(LEAF_AG, leaf_ag.at[most])
-    sent(INV_OUT, outer_view)
-    sent(INV_SWAP, inv_half)
     sent(MAT_ZRS, mat_recv.at[pl.ds(0, outer - 1)])
     sent(MAT_ZAG, mat_sum.at[:, pl.ds(0, outer - 1)])
     sent(MAT_AG, mat_ag.at[pl.ds(0, inner * nt - 1)])
     for w in range(WAVES - 1):
         sent(US + w, u_other.at[w])
         sent(UP + w, u_recv.at[w, most])
-        sent(INV_IN + w, inner_view)
         sent(X1 + w, xs.at[0, 0])
 
 
@@ -290,12 +303,12 @@
     while inner * inner * 4 <= n and n % (inner * 2) == 0:
         inner *= 2
     outer, part = n // inner, depth // (inner * nt)
-    phases = 18
+    phases = 19
     any_spec = pl.BlockSpec(memory_space=pl.ANY)
     smem = pl.BlockSpec(memory_space=pltpu.SMEM)
     found = pl.pallas_call(
         functools.partial(kernel, n, nt),
-        out_shape=jax.ShapeDtypeStruct((waves * WB, share, depth), BF16),
+        out_shape=pltpu.VMEM((waves * WB, share, depth), BF16),
         in_specs=[any_spec, smem, smem, any_spec, any_spec, smem, any_spec, any_spec, smem],
         out_specs=pl.BlockSpec(memory_space=pltpu.VMEM),
         scratch_shapes=[
@@ -304,11 +317,10 @@
             pltpu.VMEM((depth, depth), BF16),
             pltpu.VMEM((depth, count), BF16),
             pltpu.VMEM((depth, depth), BF16),
-            pltpu.VMEM((n, share, depth), BF16),
-            pltpu.VMEM((n, share, depth), BF16),
+            pltpu.VMEM((n, share + ch // nt, depth), BF16),
+            pltpu.VMEM((n, share + ch // nt, depth), BF16),
             pltpu.VMEM((n, WB, share, depth), BF16),
-            pltpu.VMEM((n, ch, depth // nt), BF16),
-            pltpu.VMEM((waves, ch, depth // nt), BF16),
+            pltpu.VMEM((WB, waves, ch, depth // nt), BF16),
             pltpu.VMEM((waves, n, ch, depth), BF16),
             pltpu.VMEM((WB * waves, count, depth), BF16),
             pltpu.VMEM((waves, n, share, depth), BF16),
@@ -316,9 +328,8 @@
             pltpu.VMEM((waves, WB, share, depth), BF16),
             pltpu.VMEM((waves, WB, count, depth), BF16),
             pltpu.VMEM((waves, count, depth), BF16),
-            pltpu.VMEM((TW * WB * WB, 128), F32),
-            pltpu.VMEM((inner * nt, TW * WB * WB, 128), F32),
-            pltpu.VMEM((inner * nt, TW, part, depth), BF16),
+            pltpu.VMEM((inner * nt, TW * part + TW * WB * WB, depth), BF16),
+            pltpu.VMEM((inner * nt, TW * part + TW * WB * WB, depth), BF16),
             pltpu.VMEM((outer, WB, WB, part // outer, depth), BF16),
             pltpu.VMEM((outer, WB, WB, part // outer, depth), BF16),
             pltpu.VMEM((WB, outer, WB, part // outer, depth), BF16),
@@ -348,7 +359,7 @@
 
     def body(*args):
         depth, count = args[3].shape[-2:]
-        if WAVES == 3 and nt == WB and n > 3 and depth % (16 * n) == 0 and depth % (128 * nt) == 0 and count % (8 * n) == 0:
+        if WAVES == 3 and nt == WB and n > 7 and depth % (16 * n) == 0 and depth % (128 * nt) == 0 and count % (8 * n) == 0:
             return fast_body(n, nt, *args)
         return general_body(*args)
 

time: 32.3 us -> 29.8 us (0.923)
  Pallas kernels: 30.7 us -> 29 us
  local copies, waits for them, and re-layouts: 1.32 us -> 0.61 us
    pallas_call x1, Pallas kernels: 30.7 us -> 29 us  [fast_body(): pl.pallas_call(functools.partial(kernel, n, nt), out_shape=pltpu.VMEM((wa...]
    unnamed x1, local copies, waits for them, and re-layouts: 1.32 us -> 0.61 us
where the time goes in v2:
time: 29.8 us; the launch traced here: 29.6 us
  Pallas kernels  29 us (97%)
  local copies, waits for them, and re-layouts  0.61 us (2%)
    pallas_call x1, Pallas kernels, fast_body(): pl.pallas_call(functools.partial(kernel, n, nt), out_shape=pltpu.VMEM((wa...  29 us
    unnamed x1, local copies, waits for them, and re-layouts  0.61 us

profile of v2, /device:TPU:0, one launch (start us, length us, event | category | flops | bytes accessed | tf_op | source)
XLA Modules:
  0.0 29.6 jit_solution(4097109828317048576)
XLA Ops:
  0.0 29.0 %shard_map.91 = bf16[4,8,256]{2,1,0:T(8,128)(2,1)S(1)} custom-call(bf16[1,1,4,256,256]{4,3,2,1,0:T(8,128)(2,1)} %tiles_h.1, s32[1,1,4]{2,1,0:T(1,128)} %src.1, s32[1,1,4]{2,1,0:T(1,128)} %dst.1, bf16[1,1,256,128]{3,2,1,0:T(8,128)(2,1)} %rhs_h.1, bf16[1,1,256,256]{3,2,1,0:T(8,128)(2,1)} %linv_h.1, s32[1,2]{1,0:T(1,128)} %lown.1, ...), custom_call_target="tpu_custom_call" | custom-call | tf_op jit(solution)/shard_map/pallas_call | solution.py:309
  29.0 0.6 %copy.11 = bf16[4,256,8]{1,2,0:T(8,128)(2,1)} copy(bf16[4,256,8]{1,2,0:T(8,128)(2,1)S(1)} %bitcast.1) | data formatting | bytes 32768

commit v3 on v2

--- a/solution.py
+++ b/solution.py
@@ -58,7 +58,7 @@
 
 def kernel(
     n, nt, tiles_h, src, dst, rhs_h, linv_h, lown, arhs_h, ainv_h, aown, out,
-    tiles, rhs, linv, arhs, ainv, own, leaf_rs, leaf_ag, inv_half, inv_ag, known, u_send, u_recv, xs,
+    tiles, rhs, linv, arhs, ainv, own, leaf_rs, leaf_ag, inv_src, inv_rs, inv_half, inv_ag, known, u_send, u_recv, xs,
     u_mine, u_other, mat_src, mat_rs, mat_send, mat_recv, mat_sum, mat_ag, lsem, ssem, rsem,
 ):
     r = lax.axis_index("rows")
@@ -108,15 +108,71 @@
     loads[0].wait()
     loads[1].wait()
     own_leaf = jnp.dot(linv[...], rhs[...], preferred_element_type=F32)
-    own[:, :share] = own_leaf.T.astype(BF16).reshape(n, share, depth)
+    own[...] = own_leaf.T.astype(BF16).reshape(n, share, depth)
+    pl.semaphore_wait(barrier, every - 1)
+
+    def push(phase, a, b, where):
+        pltpu.make_async_remote_copy(
+            src_ref=a, dst_ref=b, send_sem=ssem.at[phase], recv_sem=rsem.at[phase],
+            device_id=where, device_id_type=MESH,
+        ).start()
+
+    def rows_send(phase, make):
+        for j in others:
+            push(phase, *make(j), (j, t))
+
+    def landed(phase, view):
+        pltpu.make_async_copy(view, view, rsem.at[phase]).wait()
+
+    def sent(phase, view):
+        pltpu.make_async_copy(view, view, ssem.at[phase]).wait()
+
+    most = pl.ds(0, n - 1)
+    outer = n // inner
+    ro, ri = r // inner, lax.rem(r, inner)
+    chunk = ri * outer + ro
+    lanes_each = depth // nt
+    lanes = pl.ds(pl.multiple_of(t * lanes_each, lanes_each), lanes_each)
+
+    def rows_of(at):
+        return pl.ds(pl.multiple_of(at * ch, ch), ch)
+
+    def inv_part(j):
+        return rows_of(lax.rem(j, inner) * outer + j // inner)
+
+    inner_view = inv_ag.at[:, pl.ds(0, (inner - 1) * outer)]
+    outer_view = inv_ag.at[0, pl.ds(0, outer * nt - 1)]
+    (LEAF_RS, INV_RS, LEAF_AG, INV_OUT, _, INV_SWAP, COEF, MAT_RS, MAT_ZRS, MAT_ZAG, MAT_AG, X1, X2, INV_IN, _,
+     UP, _, US, _) = range(19)
+    def flip(v, m, size):
+        if size & (size - 1):
+            return lax.rem(v + m, size)
+        j = v
+        bit = 1
+        while bit < size:
+            if m & bit:
+                j = j + bit * (1 - 2 * lax.rem(v // bit, 2))
+            bit *= 2
+        return j
+
+    zs = [flip(ro, m, outer) for m in range(outer - 1, 0, -1)]
+    mates = [flip(ri, m, inner) for m in sorted(range(1, inner), key=lambda m: -bin(m).count('1'))]
+    near = [(i, q) for i in mates for q in (t, 1 - t)] + [(ri, 1 - t)]
+    place = ri * nt + t
+    pieces = inner * nt
+    part = depth // pieces
+    piece = part // outer
+    rows_send(LEAF_RS, lambda j: (own.at[j], leaf_rs.at[r]))
+    leaf_rs[r] = own[r]
     loads[2].wait()
     half, width = ch // nt, depth // nt
     lanes0 = pl.ds(pl.multiple_of(t * width, width), width)
     mine = ainv[:, lanes0]
     for j in range(n):
         at = (j % inner) * (n // inner) + j // inner
-        for q in range(nt):
-            own[j, share:, q * width : (q + 1) * width] = mine[at * ch + q * half : at * ch + (q + 1) * half]
+        inv_src[j] = mine[at * ch : (at + 1) * ch]
+    rows_send(INV_RS, lambda j: (inv_src.at[j], inv_rs.at[r]))
+    inv_rs[r] = inv_src[r]
     loads[4].wait()
     pieces = inner * nt
     part = depth // pieces
@@ -124,63 +180,18 @@
         for k in range(TW):
             mat_src[j, k * part : (k + 1) * part] = tiles[TW + k, j * part : (j + 1) * part]
         mat_src[j, TW * part :] = coef
-    pl.semaphore_wait(barrier, every - 1)
-
-    def push(phase, a, b, where):
-        pltpu.make_async_remote_copy(
-            src_ref=a, dst_ref=b, send_sem=ssem.at[phase], recv_sem=rsem.at[phase],
-            device_id=where, device_id_type=MESH,
-        ).start()
-
-    def rows_send(phase, make):
-        for j in others:
-            push(phase, *make(j), (j, t))
-
-    def landed(phase, view):
-        pltpu.make_async_copy(view, view, rsem.at[phase]).wait()
-
-    def sent(phase, view):
-        pltpu.make_async_copy(view, view, ssem.at[phase]).wait()
-
-    most = pl.ds(0, n - 1)
-    outer = n // inner
-    ro, ri = r // inner, lax.rem(r, inner)
-    chunk = ri * outer + ro
-    lanes_each = depth // nt
-    lanes = pl.ds(pl.multiple_of(t * lanes_each, lanes_each), lanes_each)
-
-    def rows_of(at):
-        return pl.ds(pl.multiple_of(at * ch, ch), ch)
-
-    def inv_part(j):
-        return rows_of(lax.rem(j, inner) * outer + j // inner)
-
-    inner_view = inv_ag.at[:, pl.ds(0, (inner - 1) * outer)]
-    outer_view = inv_ag.at[0, pl.ds(0, outer * nt - 1)]
-    (LEAF_RS, INV_RS, LEAF_AG, INV_OUT, _, INV_SWAP, COEF, MAT_RS, MAT_ZRS, MAT_ZAG, MAT_AG, X1, X2, INV_IN, _,
-     UP, _, US, _) = range(19)
-    zs = [lax.rem(ro + k, outer) for k in range(1, outer)]
-    near = [(lax.rem(ri + k, inner), q) for k in range(1, inner) for q in (t, 1 - t)] + [(ri, 1 - t)]
-    place = ri * nt + t
-    part = depth // (inner * nt)
-    piece = part // outer
-    rows_send(LEAF_RS, lambda j: (own.at[j], leaf_rs.at[r]))
-    leaf_rs[r] = own[r]
     for i, q in near:
         push(MAT_RS, mat_src.at[i * nt + q], mat_rs.at[place], (ro * inner + i, q))
     mat_rs[place] = mat_src[place]
     landed(LEAF_RS, leaf_rs.at[most])
     for b in range(WB):
-        leaf_ag[r, b] = leaf_rs[lown[0, b], :share]
+        leaf_ag[r, b] = leaf_rs[lown[0, b]]
     rows_send(LEAF_AG, lambda j: (leaf_ag.at[r], leaf_ag.at[r]))
 
-    def picked(owner):
-        rows = leaf_rs[owner, share:]
-        return jnp.concatenate([rows[:, q * lanes_each : (q + 1) * lanes_each] for q in range(nt)], axis=0)
-
+    landed(INV_RS, inv_rs.at[most])
     for b in range(WB):
         for w in range(WAVES - 1):
-            inv_half[b, w] = picked(aown[w * WB + b])
+            inv_half[b, w] = inv_rs[aown[w * WB + b]]
     for z in zs:
         for q in (t, 1 - t):
             push(INV_OUT, inv_half.at[q], inv_ag.at[:, chunk, :, lanes], (z * inner + ri, q))
@@ -210,14 +221,13 @@
     for z in zs:
         push(MAT_ZAG, mat_sum.at[:, ro], mat_sum.at[:, ro], (z * inner + ri, t))
 
-    landed(INV_OUT, outer_view)
-    held = pl.ds(ri * outer, outer)
-    for k in range(1, inner):
-        to = ro * inner + lax.rem(ri + k, inner)
-        push(INV_IN, inv_ag.at[:, held], inv_ag.at[:, held], (to, t))
     landed(LEAF_AG, leaf_ag.at[most])
     for b in range(WB):
         known[b] = leaf_ag[:, b].reshape(count, depth)
+    landed(INV_OUT, outer_view)
+    held = pl.ds(ri * outer, outer)
+    for i in mates:
+        push(INV_IN, inv_ag.at[:, held], inv_ag.at[:, held], (ro * inner + i, t))
     for w in (0,):
         products = []
         for k in range(w * TW, (w + 1) * TW):
@@ -282,6 +292,7 @@
 
     sent(INV_OUT, outer_view)
     sent(INV_IN, inner_view)
+    sent(INV_RS, inv_rs.at[most])
     sent(LEAF_RS, own.at[most])
     sent(MAT_RS, mat_rs.at[pl.ds(0, inner * nt - 1)])
     sent(LEAF_AG, leaf_ag.at[most])
@@ -317,9 +328,11 @@
             pltpu.VMEM((depth, depth), BF16),
             pltpu.VMEM((depth, count), BF16),
             pltpu.VMEM((depth, depth), BF16),
-            pltpu.VMEM((n, share + ch // nt, depth), BF16),
-            pltpu.VMEM((n, share + ch // nt, depth), BF16),
+            pltpu.VMEM((n, share, depth), BF16),
+            pltpu.VMEM((n, share, depth), BF16),
             pltpu.VMEM((n, WB, share, depth), BF16),
+            pltpu.VMEM((n, ch, depth // nt), BF16),
+            pltpu.VMEM((n, ch, depth // nt), BF16),
             pltpu.VMEM((WB, waves, ch, depth // nt), BF16),
             pltpu.VMEM((waves, n, ch, depth), BF16),
             pltpu.VMEM((WB * waves, count, depth), BF16),

time: 29.8 us -> 29.5 us (0.990)
  Pallas kernels: 29 us -> 28.7 us
where the time goes in v3:
time: 29.5 us; the launch traced here: 29.3 us
  Pallas kernels  28.7 us (97%)
  local copies, waits for them, and re-layouts  0.61 us (2%)
    pallas_call x1, Pallas kernels, fast_body(): pl.pallas_call(functools.partial(kernel, n, nt), out_shape=pltpu.VMEM((wa...  28.7 us
    unnamed x1, local copies, waits for them, and re-layouts  0.61 us

profile of v3, /device:TPU:0, one launch (start us, length us, event | category | flops | bytes accessed | tf_op | source)
XLA Modules:
  0.0 29.3 jit_solution(12572326860740593238)
XLA Ops:
  0.0 28.7 %shard_map.91 = bf16[4,8,256]{2,1,0:T(8,128)(2,1)S(1)} custom-call(bf16[1,1,4,256,256]{4,3,2,1,0:T(8,128)(2,1)} %tiles_h.1, s32[1,1,4]{2,1,0:T(1,128)} %src.1, s32[1,1,4]{2,1,0:T(1,128)} %dst.1, bf16[1,1,256,128]{3,2,1,0:T(8,128)(2,1)} %rhs_h.1, bf16[1,1,256,256]{3,2,1,0:T(8,128)(2,1)} %linv_h.1, s32[1,2]{1,0:T(1,128)} %lown.1, ...), custom_call_target="tpu_custom_call" | custom-call | tf_op jit(solution)/shard_map/pallas_call | solution.py:320
  28.7 0.6 %copy.11 = bf16[4,256,8]{1,2,0:T(8,128)(2,1)} copy(bf16[4,256,8]{1,2,0:T(8,128)(2,1)S(1)} %bitcast.1) | data formatting | bytes 32768

commit v4 on v3

--- a/solution.py
+++ b/solution.py
@@ -140,8 +140,7 @@
     def inv_part(j):
         return rows_of(lax.rem(j, inner) * outer + j // inner)
 
-    inner_view = inv_ag.at[:, pl.ds(0, (inner - 1) * outer)]
-    outer_view = inv_ag.at[0, pl.ds(0, outer * nt - 1)]
+    in_views = (inv_ag.at[0, pl.ds(0, inner - 1)], inv_ag.at[1, :, pl.ds(0, outer - 1)])
     (LEAF_RS, INV_RS, LEAF_AG, INV_OUT, _, INV_SWAP, COEF, MAT_RS, MAT_ZRS, MAT_ZAG, MAT_AG, X1, X2, INV_IN, _,
      UP, _, US, _) = range(19)
     def flip(v, m, size):
@@ -194,9 +193,12 @@
             inv_half[b, w] = inv_rs[aown[w * WB + b]]
     for z in zs:
         for q in (t, 1 - t):
-            push(INV_OUT, inv_half.at[q], inv_ag.at[:, chunk, :, lanes], (z * inner + ri, q))
-    push(INV_OUT, inv_half.at[1 - t], inv_ag.at[:, chunk, :, lanes], (r, 1 - t))
-    inv_ag[:, chunk, :, lanes] = inv_half[t]
+            push(INV_OUT, inv_half.at[q, 0], inv_ag.at[0, ri, ro, :, lanes], (z * inner + ri, q))
+    push(INV_OUT, inv_half.at[1 - t, 0], inv_ag.at[0, ri, ro, :, lanes], (r, 1 - t))
+    for i, q in near:
+        push(INV_OUT + 1, inv_half.at[q, 1], inv_ag.at[1, ri, ro, :, lanes], (ro * inner + i, q))
+    for w in range(WAVES - 1):
+        inv_ag[w, ri, ro, :, lanes] = inv_half[t, w]
     landed(MAT_RS, mat_rs.at[pl.ds(0, inner * nt - 1)])
     slots = [[jnp.zeros((part, depth), F32) for s in range(WB)] for b in range(WB)]
     for j in range(inner * nt):
@@ -216,6 +218,9 @@
 
     loads[3].wait()
     arhs_t = arhs[...].astype(F32).T
+    landed(INV_OUT, inv_rs.at[pl.ds(0, outer * nt - 1)])
+    for i in mates:
+        push(INV_IN, inv_ag.at[0, ri], inv_ag.at[0, ri], (ro * inner + i, t))
     landed(MAT_ZRS, mat_recv.at[pl.ds(0, outer - 1)])
     mat_sum[:, ro] = jnp.sum(mat_recv[...].astype(F32), axis=0).astype(BF16)
     for z in zs:
@@ -224,10 +229,6 @@
     landed(LEAF_AG, leaf_ag.at[most])
     for b in range(WB):
         known[b] = leaf_ag[:, b].reshape(count, depth)
-    landed(INV_OUT, outer_view)
-    held = pl.ds(ri * outer, outer)
-    for i in mates:
-        push(INV_IN, inv_ag.at[:, held], inv_ag.at[:, held], (ro * inner + i, t))
     for w in (0,):
         products = []
         for k in range(w * TW, (w + 1) * TW):
@@ -264,6 +265,9 @@
         u_send[w] = u.reshape(n, share, depth).astype(BF16)
         rows_send(UP + w, lambda j: (u_send.at[w, j], u_recv.at[w, r]))
         u_recv[w, r] = u_send[w, r]
+    landed(INV_OUT + 1, inv_rs.at[pl.ds(0, inner * nt - 1)])
+    for z in zs:
+        push(INV_IN + 1, inv_ag.at[1, :, ro], inv_ag.at[1, :, ro], (z * inner + ri, t))
     landed(MAT_ZAG, mat_sum.at[:, pl.ds(0, outer - 1)])
     for i, q in near:
         push(MAT_AG, mat_sum.at[q], mat_ag.at[place], (ro * inner + i, q))
@@ -275,11 +279,12 @@
 
     landed(UP, u_recv.at[0, most])
     y = jnp.sum(u_recv[0].astype(F32), axis=0)
-    landed(INV_IN, inner_view)
+    landed(INV_IN, in_views[0])
     solve(0, y)
     landed(UP + 1, u_recv.at[1, most])
     y = jnp.sum(u_recv[1].astype(F32), axis=0)
     landed(MAT_AG, mat_ag.at[pl.ds(0, inner * nt - 1)])
+    landed(INV_IN + 1, in_views[1])
     landed(X1, xs.at[0, 0])
     for s in range(WB):
         mat = mat_ag[:, :, s].reshape(depth, depth)
@@ -290,8 +295,8 @@
         for b in range(WB):
             out[w * WB + b] = xs[w, b]
 
-    sent(INV_OUT, outer_view)
-    sent(INV_IN, inner_view)
+    sent(INV_OUT, inv_rs.at[pl.ds(0, outer * nt - 1)])
+    sent(INV_OUT + 1, inv_rs.at[pl.ds(0, inner * nt - 1)])
     sent(INV_RS, inv_rs.at[most])
     sent(LEAF_RS, own.at[most])
     sent(MAT_RS, mat_rs.at[pl.ds(0, inner * nt - 1)])
@@ -302,6 +307,7 @@
     for w in range(WAVES - 1):
         sent(US + w, u_other.at[w])
         sent(UP + w, u_recv.at[w, most])
+        sent(INV_IN + w, in_views[w])
         sent(X1 + w, xs.at[0, 0])
 
 
@@ -334,7 +340,7 @@
             pltpu.VMEM((n, ch, depth // nt), BF16),
             pltpu.VMEM((n, ch, depth // nt), BF16),
             pltpu.VMEM((WB, waves, ch, depth // nt), BF16),
-            pltpu.VMEM((waves, n, ch, depth), BF16),
+            pltpu.VMEM((waves, inner, outer, ch, depth), BF16),
             pltpu.VMEM((WB * waves, count, depth), BF16),
             pltpu.VMEM((waves, n, share, depth), BF16),
             pltpu.VMEM((waves, n, share, depth), BF16),

time: 29.5 us -> 29.5 us (level)
  no operation moved by 1% of the time
where the time goes in v4:
time: 29.5 us; the launch traced here: 29.4 us
  Pallas kernels  28.7 us (97%)
  local copies, waits for them, and re-layouts  0.61 us (2%)
    pallas_call x1, Pallas kernels, fast_body(): pl.pallas_call(functools.partial(kernel, n, nt), out_shape=pltpu.VMEM((wa...  28.7 us
    unnamed x1, local copies, waits for them, and re-layouts  0.61 us

profile of v4, /device:TPU:0, one launch (start us, length us, event | category | flops | bytes accessed | tf_op | source)
XLA Modules:
  0.0 29.4 jit_solution(318565582721015875)
XLA Ops:
  0.0 28.7 %shard_map.91 = bf16[4,8,256]{2,1,0:T(8,128)(2,1)S(1)} custom-call(bf16[1,1,4,256,256]{4,3,2,1,0:T(8,128)(2,1)} %tiles_h.1, s32[1,1,4]{2,1,0:T(1,128)} %src.1, s32[1,1,4]{2,1,0:T(1,128)} %dst.1, bf16[1,1,256,128]{3,2,1,0:T(8,128)(2,1)} %rhs_h.1, bf16[1,1,256,256]{3,2,1,0:T(8,128)(2,1)} %linv_h.1, s32[1,2]{1,0:T(1,128)} %lown.1, ...), custom_call_target="tpu_custom_call" | custom-call | tf_op jit(solution)/shard_map/pallas_call | solution.py:326
  28.7 0.6 %copy.11 = bf16[4,256,8]{1,2,0:T(8,128)(2,1)} copy(bf16[4,256,8]{1,2,0:T(8,128)(2,1)S(1)} %bitcast.1) | data formatting | bytes 32768
